TPU v7x, 32 devices: a whole 2x2x4 slice. The times are simulated.
32 devices in a mesh: section: 4 (over y, x), expert: 8 (over z, core).
Axes of the slice: x: 2, y: 2, z: 4, core: 2. Of those that a mesh axis runs over, the one named last changes fastest.
Arguments:
- forward_input: bfloat16 [4, 576, 4096], P('section', 'expert'), may hold values from -6 to 6
- backward_cotangent: bfloat16 [4, 576, 4096], P('section', 'expert'), may hold values from -6 to 6
- saved_input: bfloat16 [4, 576, 4096], P('section', 'expert'), may hold values from -6 to 6
- saved_hidden: bfloat16 [4, 8, 360, 1536], P('section', 'expert'), may hold values from -8 to 8
- norm_gain: float32 [4, 4096], P('section'), may hold values from 0.5 to 2
- forward_experts: int32 [4, 576, 4], P('section', 'expert'), may hold values from 0 to 7, all different within a row; in each aligned block of 72 rows (0 to 71, 72 to 143, ..., all dimensions but the last counted through in order) at most 45 rows name the same one
- forward_gates: float32 [4, 576, 4], P('section', 'expert'), may hold values from 0.05 to 1
- backward_experts: int32 [4, 576, 4], P('section', 'expert'), may hold values from 0 to 7, all different within a row; in each aligned block of 72 rows (0 to 71, 72 to 143, ..., all dimensions but the last counted through in order) at most 45 rows name the same one
- backward_gates: float32 [4, 576, 4], P('section', 'expert'), may hold values from 0.05 to 1
- gate_up_weight: bfloat16 [4, 8, 4096, 1536], P('section', 'expert'), may hold values from -0.09375 to 0.09375
- down_weight: bfloat16 [4, 8, 768, 4096], P('section', 'expert'), may hold values from -0.21875 to 0.21875
Outputs:
- forward_output: bfloat16 [4, 576, 4096], P('section', 'expert')
- input_gradient: bfloat16 [4, 576, 4096], P('section', 'expert')
Inputs may be any that keep to these rules, and one draw needn't show every extreme that they name: `forward_experts`: each token names 4 distinct experts. In the rows of one device (aligned blocks of 72 tokens) no expert is named by more than 45 entries, and in some device's rows some expert is named by exactly 45. `backward_experts`: same law as forward_experts, drawn independently.
All inputs are finite; a program needn't handle non-finite values.
Results may differ from a plain program's by a relative error of at most 0.0054.
Values may be sent and summed in bfloat16 or wider, within the bound.
A program may use at most 128 MiB of HBM per device.

v0:
```python
import jax
import jax.numpy as jnp
from jax import lax
from jax.sharding import PartitionSpec as P

EPSILON = 1e-06


def passed_along(value, axis, steps):
    count = lax.axis_size(axis)
    initial, last = (max(0, -steps), min(count, count - steps))
    return lax.ppermute(value, axis, [(source, source + steps) for source in range(initial, last)])


def norm_scale(values, gain_row):
    widened = values.astype(jnp.float32)
    inverse = lax.rsqrt(jnp.mean(widened * widened, axis=-1, keepdims=True) + EPSILON)
    return widened * inverse * gain_row


def dense_weights(expert_ids, gates, expert_count):
    weights = gates / jnp.sum(gates, axis=-1, keepdims=True)
    onehot = expert_ids[:, :, None] == jnp.arange(expert_count, dtype=jnp.int32)[None, None, :]
    return jnp.sum(jnp.where(onehot, weights[:, :, None], 0.0), axis=1)


def local(
    forward_input,
    backward_cotangent,
    saved_input,
    saved_hidden,
    norm_gain,
    forward_experts,
    forward_gates,
    backward_experts,
    backward_gates,
    gate_up_weight,
    down_weight,
):
    peer_count = lax.axis_size("expert")
    me = lax.axis_index("expert")
    table = jnp.concatenate(
        [
            dense_weights(forward_experts[0], forward_gates[0], peer_count),
            dense_weights(backward_experts[0], backward_gates[0], peer_count),
        ],
        axis=1,
    )
    tables = lax.all_gather(table, "expert", axis=0, tiled=True)
    weight_f = lax.dynamic_slice_in_dim(tables, me, 1, axis=1)
    weight_b = lax.dynamic_slice_in_dim(tables, peer_count + me, 1, axis=1)
    moved_input, moved_cotangent = passed_along((forward_input, backward_cotangent), "section", 1)
    is_first = lax.axis_index("section") == 0
    layer_in = jnp.where(is_first, forward_input, moved_input)[0]
    cotangent = jnp.where(is_first, backward_cotangent, moved_cotangent)[0]
    token_count = layer_in.shape[0]
    slot_total = saved_hidden.shape[2]
    capacity = slot_total // peer_count
    gain_row = norm_gain[0]
    weight_in = gate_up_weight[0, 0]
    weight_down = down_weight[0, 0]
    hidden_width = weight_down.shape[0]
    normed = norm_scale(layer_in, gain_row).astype(jnp.bfloat16)
    all_normed = lax.all_gather(normed, "expert", axis=0, tiled=True)
    all_cotangent = lax.all_gather(cotangent, "expert", axis=0, tiled=True)
    projected = jnp.dot(all_normed, weight_in, preferred_element_type=jnp.float32)
    hidden = (jax.nn.silu(projected[:, :hidden_width]) * projected[:, hidden_width:]).astype(
        jnp.bfloat16
    )
    served = jnp.dot(hidden, weight_down, preferred_element_type=jnp.float32)
    served = (served * weight_f).astype(jnp.bfloat16)
    mixture = lax.psum_scatter(served, "expert", scatter_dimension=0, tiled=True)
    forward_output = (layer_in.astype(jnp.float32) + mixture.astype(jnp.float32)).astype(
        jnp.bfloat16
    )
    routed = (weight_b > 0.0).reshape(peer_count, token_count)
    slot = jnp.cumsum(routed.astype(jnp.int32), axis=1) - 1
    spread = (
        (slot[:, :, None] == jnp.arange(capacity, dtype=jnp.int32)[None, None, :])
        & routed[:, :, None]
    ).astype(jnp.bfloat16)
    saved = jnp.einsum(
        "jts,jsf->jtf",
        spread,
        saved_hidden[0, 0].reshape(peer_count, capacity, -1),
        preferred_element_type=jnp.float32,
    ).reshape(peer_count * token_count, -1)
    scaled = (weight_b * all_cotangent.astype(jnp.float32)).astype(jnp.bfloat16)
    grad_hidden = lax.dot_general(
        scaled, weight_down, (((1,), (1,)), ((), ())), preferred_element_type=jnp.float32
    )
    gate, up = (saved[:, :hidden_width], saved[:, hidden_width:])
    sig = jax.nn.sigmoid(gate)
    grad_both = jnp.concatenate(
        [grad_hidden * up * sig * (1.0 + gate * (1.0 - sig)), grad_hidden * gate * sig], axis=1
    ).astype(jnp.bfloat16)
    grads = lax.dot_general(
        grad_both, weight_in, (((1,), (1,)), ((), ())), preferred_element_type=jnp.float32
    ).astype(jnp.bfloat16)
    grad_normed = lax.psum_scatter(grads, "expert", scatter_dimension=0, tiled=True).astype(
        jnp.float32
    )

    def apply_norm(inputs):
        return norm_scale(inputs, gain_row)

    primal, pullback = jax.vjp(apply_norm, saved_input[0].astype(jnp.float32))
    input_gradient = (cotangent.astype(jnp.float32) + pullback(grad_normed)[0]).astype(jnp.bfloat16)
    return (forward_output[None], input_gradient[None])


def solution(mesh):
    row = P("section", "expert", None)
    block = P("section", "expert", None, None)
    in_specs = (row, row, row, block, P("section", None), row, row, row, row, block, block)
    return jax.shard_map(local, mesh=mesh, in_specs=in_specs, out_specs=(row, row), check_vma=False)
```

profile of v0, /device:TPU:0, one launch (start us, length us, event | category | flops | bytes accessed | tf_op | source)
XLA Modules:
  0.0 298.4 jit_solution(10791374151857974960)
XLA Ops:
  7.3 5.0 %collective-permute-start.1 = (bf16[1,72,4096]{2,1,0:T(8,128)(2,1)}, bf16[1,72,4096]{2,1,0:T(8,128)(2,1)S(1)}, u32[]{:S(2)}, u32[]{:S(2)}) collective-permute-start(bf16[1,72,4096]{2,1,0:T(8,128)(2,1)} %param.12), channel_id=1, source_target_pairs={{0,8},{8,16},{16,24},{1,9},{9,17},{17,25},{2,10},{10,18},{18,26},{... | collective-permute-start | bytes 1769480 | tf_op jit(solution)/shard_map/ppermute | solution.py:12
  12.3 12.8 %collective-permute-done.1 = bf16[1,72,4096]{2,1,0:T(8,128)(2,1)S(1)} collective-permute-done((bf16[1,72,4096]{2,1,0:T(8,128)(2,1)}, bf16[1,72,4096]{2,1,0:T(8,128)(2,1)S(1)}, u32[]{:S(2)}, u32[]{:S(2)}) %collective-permute-start.1) | collective-permute-done | bytes 589856 | tf_op jit(solution)/shard_map/ppermute | solution.py:12
  25.1 2.0 broadcast_select_fusion
  27.3 14.3 %all-gather.1 = f32[8,72,16]{1,2,0:T(8,128)S(1)} all-gather(f32[1,72,16]{1,2,0:T(8,128)S(1)} %maximum_bitcast_fusion), channel_id=1, replica_groups=mesh['section'=4,'expert'=8] {'expert'}, dimensions={0}, use_global_device_ids=true | all-gather | bytes 41472 | tf_op jit(solution)/shard_map/all_gather | solution.py:49
  41.7 0.3 reshape_squeeze.3
  42.1 0.1 reshape.92
  42.2 0.2 reduce_window_sum.11
  42.5 2.4 fusion.34
  44.9 35.2 %all-gather.7.cloned.1.call-done = bf16[1,576,4096]{2,1,0:T(8,128)(2,1)} async-done(((bf16[1,72,4096]{2,1,0:T(8,128)(2,1)}), bf16[1,576,4096]{2,1,0:T(8,128)(2,1)}) %all-gather.7.cloned.1.call-update) | async-done | bytes 4718608 | tf_op jit(solution)/shard_map/all_gather | solution.py:65
  80.1 9.4 %fusion.16 = (bf16[576,768]{1,0:T(8,128)(2,1)S(1)}, bf16[576,768]{1,0:T(8,128)(2,1)S(1)}) fusion(f32[576,1536]{1,0:T(8,128)} %bitcast.55, bf16[1,1,768,4096]{3,2,1,0:T(8,128)(2,1)} %param.21, bf16[1,576,4096]{2,1,0:T(8,128)(2,1)} %all-gather.7.cloned.1.call-done, f32[576]{0:T(1024)S(1)} %get-tuple-element.4), kind=kOutput, calls=%fused_computation.16 | convolution fusion | flops 3636707328 | bytes 16320768 | tf_op jit(solution)/shard_map/dot_general | solution.py:89
  89.6 18.4 %fusion.8 = bf16[576,4096]{1,0:T(8,128)(2,1)} fusion(bf16[1,1,4096,1536]{3,2,1,0:T(8,128)(2,1)} %param.20, bf16[576,768]{1,0:T(8,128)(2,1)S(1)} %get-tuple-element.9, bf16[576,768]{1,0:T(8,128)(2,1)S(1)} %get-tuple-element.8), kind=kOutput, calls=%fused_computation.10 | convolution fusion | flops 7253655552 | bytes 19070976 | tf_op jit(solution)/shard_map/dot_general | solution.py:97
  108.0 1.0 copy-done.3
  109.0 3.4 %collective-permute-start = (bf16[1,72,4096]{2,1,0:T(8,128)(2,1)S(1)}, bf16[1,72,4096]{2,1,0:T(8,128)(2,1)S(1)}, u32[]{:S(2)}, u32[]{:S(2)}) collective-permute-start(bf16[1,72,4096]{2,1,0:T(8,128)(2,1)S(1)} %copy-done.3), channel_id=1, source_target_pairs={{0,8},{8,16},{16,24},{1,9},{9,17},{17,25},{2,10},{10,18},{18,26},{... | collective-permute-start | bytes 1769480 | tf_op jit(solution)/shard_map/ppermute | solution.py:12
  112.4 12.9 %collective-permute-done = bf16[1,72,4096]{2,1,0:T(8,128)(2,1)S(1)} collective-permute-done((bf16[1,72,4096]{2,1,0:T(8,128)(2,1)S(1)}, bf16[1,72,4096]{2,1,0:T(8,128)(2,1)S(1)}, u32[]{:S(2)}, u32[]{:S(2)}) %collective-permute-start) | collective-permute-done | bytes 589856 | tf_op jit(solution)/shard_map/ppermute | solution.py:12
  125.3 0.3 fusion.23
  125.6 36.1 %reduce-scatter.5.cloned.1.call-done = bf16[72,4096]{1,0:T(8,128)(2,1)} async-done(((bf16[576,4096]{1,0:T(8,128)(2,1)}), bf16[72,4096]{1,0:T(8,128)(2,1)}) %reduce-scatter.5.cloned.1.call-update) | async-done | bytes 589840 | tf_op jit(solution)/shard_map/reduce_scatter | solution.py:100
  161.7 1.4 fusion.27
  163.2 2.6 fusion.32
  165.9 0.2 reduce-scatter.3.cloned.1.call-start
  166.1 50.0 %all-gather.5.cloned.1.call-done = bf16[576,4096]{1,0:T(8,128)(2,1)} async-done(((bf16[72,4096]{1,0:T(8,128)(2,1)}), bf16[576,4096]{1,0:T(8,128)(2,1)}) %all-gather.5.cloned.1.call-update) | async-done | bytes 4718608 | tf_op jit(solution)/shard_map/all_gather | solution.py:64
  216.1 11.5 %fusion.2 = f32[576,1536]{1,0:T(8,128)S(1)} fusion(bf16[576,4096]{1,0:T(8,128)(2,1)} %all-gather.5.cloned.1.call-done, bf16[1,1,4096,1536]{3,2,1,0:T(8,128)(2,1)} %param.20), kind=kOutput, calls=%fused_computation.2 | convolution fusion | flops 7247757312 | bytes 20840448 | tf_op jit(solution)/shard_map/dot_general | solution.py:66
  227.5 8.4 %multiply_convert_fusion = bf16[576,4096]{1,0:T(8,128)(2,1)} fusion(bf16[1,1,768,4096]{3,2,1,0:T(8,128)(2,1)} %param.21, f32[576]{0:T(1024)S(1)} %get-tuple-element.5, f32[576,1536]{1,0:T(8,128)S(1)} %fusion.2), kind=kOutput, calls=%fused_computation.6 | convolution fusion | flops 3631251456 | bytes 14551296 | tf_op jit(solution)/shard_map/dot_general | solution.py:70
  235.9 53.9 %reduce-scatter.3.cloned.1.call-done = bf16[72,4096]{1,0:T(8,128)(2,1)} async-done(((bf16[576,4096]{1,0:T(8,128)(2,1)}), bf16[72,4096]{1,0:T(8,128)(2,1)}) %reduce-scatter.3.cloned.1.call-update) | async-done | bytes 589840 | tf_op jit(solution)/shard_map/reduce_scatter | solution.py:72
  289.9 2.0 fusion.31
  (38 shorter events, 0.5 us)
Async XLA Ops:
  7.2 20.0 %copy-start.5 = (f32[1,72,4]{1,2,0:T(4,128)S(1)}, f32[1,72,4]{1,2,0:T(4,128)}, u32[]{:S(2)}) copy-start(f32[1,72,4]{1,2,0:T(4,128)} %param.19) | copy-start | bytes 3460
  7.2 20.0 %copy-start.6 = (f32[1,72,4]{1,2,0:T(4,128)S(1)}, f32[1,72,4]{1,2,0:T(4,128)}, u32[]{:S(2)}) copy-start(f32[1,72,4]{1,2,0:T(4,128)} %param.17) | copy-start | bytes 3460
  7.2 20.1 %copy-start.7 = (s32[1,72,4]{1,2,0:T(4,128)S(1)}, s32[1,72,4]{1,2,0:T(4,128)}, u32[]{:S(2)}) copy-start(s32[1,72,4]{1,2,0:T(4,128)} %param.18) | copy-start | bytes 3460
  7.2 20.1 %copy-start.8 = (s32[1,72,4]{1,2,0:T(4,128)S(1)}, s32[1,72,4]{1,2,0:T(4,128)}, u32[]{:S(2)}) copy-start(s32[1,72,4]{1,2,0:T(4,128)} %param.16) | copy-start | bytes 3460
  7.2 34.5 %copy-start.2 = (bf16[1,1,360,1536]{3,2,1,0:T(8,128)(2,1)S(1)}, bf16[1,1,360,1536]{3,2,1,0:T(8,128)(2,1)}, u32[]{:S(2)}) copy-start(bf16[1,1,360,1536]{3,2,1,0:T(8,128)(2,1)} %param.14) | copy-start | bytes 3317764
  7.2 72.9 %all-gather.7.cloned.1.call-start = ((), (), s32[]{:S(2)}) async-start(), calls=%async_computation.5 | async-start | bytes 5308416 | tf_op jit(solution)/shard_map/all_gather | solution.py:65
  7.3 17.9 %collective-permute-start.1 = (bf16[1,72,4096]{2,1,0:T(8,128)(2,1)}, bf16[1,72,4096]{2,1,0:T(8,128)(2,1)S(1)}, u32[]{:S(2)}, u32[]{:S(2)}) collective-permute-start(bf16[1,72,4096]{2,1,0:T(8,128)(2,1)} %param.12), channel_id=1, source_target_pairs={{0,8},{8,16},{16,24},{1,9},{9,17},{17,25},{2,10},{10,18},{18,26},{... | collective-permute-start | bytes 1769480 | tf_op jit(solution)/shard_map/ppermute | solution.py:12
  27.1 134.6 %reduce-scatter.5.cloned.1.call-start = ((), (), s32[]{:S(2)}) async-start(), calls=%async_computation.4 | async-start | bytes 5308416 | tf_op jit(solution)/shard_map/reduce_scatter | solution.py:100
  107.9 1.1 copy-start.3
  107.9 53.8 %copy-start.1 = (bf16[1,72,4096]{2,1,0:T(8,128)(2,1)S(1)}, bf16[1,72,4096]{2,1,0:T(8,128)(2,1)}, u32[]{:S(2)}) copy-start(bf16[1,72,4096]{2,1,0:T(8,128)(2,1)} %param.13) | copy-start | bytes 1769476
  107.9 53.8 %copy-start.4 = (f32[1,4096]{1,0:T(1,128)S(1)}, f32[1,4096]{1,0:T(1,128)}, u32[]{:S(2)}) copy-start(f32[1,4096]{1,0:T(1,128)} %param.15) | copy-start | bytes 49156
  108.0 55.2 %copy-start = (bf16[1,72,4096]{2,1,0:T(8,128)(2,1)S(1)}, bf16[1,72,4096]{2,1,0:T(8,128)(2,1)}, u32[]{:S(2)}) copy-start(bf16[1,72,4096]{2,1,0:T(8,128)(2,1)} %broadcast_select_fusion) | copy-start | bytes 1769476
  108.0 108.1 %all-gather.5.cloned.1.call-start = ((), (), s32[]{:S(2)}) async-start(), calls=%async_computation.2 | async-start | bytes 5308416 | tf_op jit(solution)/shard_map/all_gather | solution.py:64
  109.0 16.3 %collective-permute-start = (bf16[1,72,4096]{2,1,0:T(8,128)(2,1)S(1)}, bf16[1,72,4096]{2,1,0:T(8,128)(2,1)S(1)}, u32[]{:S(2)}, u32[]{:S(2)}) collective-permute-start(bf16[1,72,4096]{2,1,0:T(8,128)(2,1)S(1)} %copy-done.3), channel_id=1, source_target_pairs={{0,8},{8,16},{16,24},{1,9},{9,17},{17,25},{2,10},{10,18},{18,26},{... | collective-permute-start | bytes 1769480 | tf_op jit(solution)/shard_map/ppermute | solution.py:12
  165.9 124.0 %reduce-scatter.3.cloned.1.call-start = ((), (), s32[]{:S(2)}) async-start(), calls=%async_computation.3 | async-start | bytes 5308416 | tf_op jit(solution)/shard_map/reduce_scatter | solution.py:72
Sparse Core Ops, SparseCore 0:
  27.2 52.8 all-gather.6
  108.1 53.6 reduce-scatter.4
  166.0 50.0 all-gather.4
  236.1 53.7 reduce-scatter.2
where the time goes:
time: 299 us; the launch traced here: 298 us
  waiting for transfers between devices  201 us (67%)
  matrix products  50 us (17%)
  blocking collectives  14.3 us (5%)
  between operations  14 us (5%)
  starting transfers between devices  8.75 us (3%)
  other arithmetic  8.72 us (3%)
    reduce_scatter x1, waiting for transfers between devices, local(): lax.psum_scatter(served, 'expert', scatter_dimension=0, tiled=True)  53.9 us
    all_gather x1, waiting for transfers between devices, local(): all_normed = lax.all_gather(normed, 'expert', axis=0, tiled=True)  50 us
    reduce_scatter x1, waiting for transfers between devices, local(): lax.psum_scatter(grads, 'expert', scatter_dimension=0, tiled=True)  36.1 us
    all_gather x1, waiting for transfers between devices, local(): all_cotangent = lax.all_gather(cotangent, 'expert', axis=0, tiled=True)  35.2 us
    ppermute x2, waiting for transfers between devices, passed_along(): lax.ppermute(value, axis, [(source, source + steps) for source in range(i...  25.8 us
    dot_general x1, matrix products, local(): lax.dot_general(grad_both, weight_in, (((1,), (1,)), ((), ())), preferred...  18.4 us
    all_gather x1, blocking collectives, local(): tables = lax.all_gather(table, 'expert', axis=0, tiled=True)  14.3 us
    dot_general x1, matrix products, local(): jnp.dot(all_normed, weight_in, preferred_element_type=jnp.float32)  11.5 us
  transfers between devices with their start and end apart: 6, of which 6 were waited for; matrix products, arithmetic and copies ran while one was open for 1% of the time, Pallas kernels for 0%

commit v1 on v0

--- a/solution.py
+++ b/solution.py
@@ -4,6 +4,22 @@
 from jax.sharding import PartitionSpec as P
 
 EPSILON = 1e-06
+
+
+def collect(x, axis, dim):
+    ways, here, hop = (lax.axis_size(axis), lax.axis_index(axis), x.shape[dim])
+    shape = [n * ways if d == dim else n for d, n in enumerate(x.shape)]
+    full = lax.dynamic_update_slice_in_dim(jnp.zeros(shape, x.dtype), x, here * hop, axis=dim)
+    going_up = going_down = x
+    for far in range(1, ways // 2 + 1):
+        going_up = lax.ppermute(going_up, axis, [(d, (d + 1) % ways) for d in range(ways)])
+        full = lax.dynamic_update_slice_in_dim(full, going_up, (here - far) % ways * hop, axis=dim)
+        if 2 * far < ways:
+            going_down = lax.ppermute(going_down, axis, [(d, (d - 1) % ways) for d in range(ways)])
+            full = lax.dynamic_update_slice_in_dim(
+                full, going_down, (here + far) % ways * hop, axis=dim
+            )
+    return full
 
 
 def passed_along(value, axis, steps):
@@ -61,7 +77,7 @@
     weight_down = down_weight[0, 0]
     hidden_width = weight_down.shape[0]
     normed = norm_scale(layer_in, gain_row).astype(jnp.bfloat16)
-    all_normed = lax.all_gather(normed, "expert", axis=0, tiled=True)
+    all_normed = collect(normed, "expert", 0)
     all_cotangent = lax.all_gather(cotangent, "expert", axis=0, tiled=True)
     projected = jnp.dot(all_normed, weight_in, preferred_element_type=jnp.float32)
     hidden = (jax.nn.silu(projected[:, :hidden_width]) * projected[:, hidden_width:]).astype(

time: 299 us -> 277 us (0.926)
  waiting for transfers between devices: 201 us -> 125 us
  blocking collectives: 14.3 us -> 47.7 us
  starting transfers between devices: 8.75 us -> 19.3 us
  local copies, waits for them, and re-layouts: 1.55 us -> 10.5 us
  other arithmetic: 8.72 us -> 11.9 us
    all_gather x1 -> x0, waiting for transfers between devices: 50 us -> none  [local(): all_normed = lax.all_gather(normed, 'expert', axis=0, tiled=True)]
    all_gather x1, waiting for transfers between devices: 35.2 us -> 0.01 us  [local(): all_cotangent = lax.all_gather(cotangent, 'expert', axis=0, tiled=True)]
    all_gather x1, blocking collectives: 14.3 us -> 47.7 us  [local(): tables = lax.all_gather(table, 'expert', axis=0, tiled=True)]
    reduce_scatter x1, waiting for transfers between devices: 53.9 us -> 20.9 us  [local(): lax.psum_scatter(served, 'expert', scatter_dimension=0, tiled=True)]
    ppermute x0 -> x7, waiting for transfers between devices: none -> 32.1 us  [the longest x4 32.1 us: collect(): lax.ppermute(going_up, axis, [(d, (d + 1) % ways) for d in range(ways)])]
    reduce_scatter x1, waiting for transfers between devices: 36.1 us -> 53.6 us  [local(): lax.psum_scatter(grads, 'expert', scatter_dimension=0, tiled=True)]
    ppermute x0 -> x7, starting transfers between devices: none -> 10.7 us  [the longest x3 10.3 us: collect(): lax.ppermute(going_down, axis, [(d, (d - 1) % ways) for d in range(ways)])]
    ppermute x2, waiting for transfers between devices: 25.8 us -> 18.5 us  [passed_along(): lax.ppermute(value, axis, [(source, source + steps) for source in range(i...]
  transfers between devices with their start and end apart: 6 -> 12, of which waited for: 6 -> 7; matrix products, arithmetic and copies ran while one was open for 1% -> 24% of each run, Pallas kernels for 0% -> 0%
where the time goes in v1:
time: 277 us
  waiting for transfers between devices  125 us (45%)
  matrix products  48 us (17%)
  blocking collectives  47.7 us (17%)
  starting transfers between devices  19.3 us (7%)
  between operations  14.1 us (5%)
  other arithmetic  11.9 us (4%)
  local copies, waits for them, and re-layouts  10.5 us (4%)
    reduce_scatter x1, waiting for transfers between devices, local(): lax.psum_scatter(grads, 'expert', scatter_dimension=0, tiled=True)  53.6 us
    all_gather x1, blocking collectives, local(): tables = lax.all_gather(table, 'expert', axis=0, tiled=True)  47.7 us
    ppermute x4, waiting for transfers between devices, collect(): lax.ppermute(going_up, axis, [(d, (d + 1) % ways) for d in range(ways)])  32.1 us
    reduce_scatter x1, waiting for transfers between devices, local(): lax.psum_scatter(served, 'expert', scatter_dimension=0, tiled=True)  20.9 us
    ppermute x2, waiting for transfers between devices, passed_along(): lax.ppermute(value, axis, [(source, source + steps) for source in range(i...  18.5 us
    dot_general x1, matrix products, local(): lax.dot_general(grad_both, weight_in, (((1,), (1,)), ((), ())), preferred...  18.5 us
    dot_general x1, matrix products, local(): jnp.dot(all_normed, weight_in, preferred_element_type=jnp.float32)  12.1 us
    ppermute x3, starting transfers between devices, collect(): lax.ppermute(going_down, axis, [(d, (d - 1) % ways) for d in range(ways)])  10.3 us
  transfers between devices with their start and end apart: 12, of which 7 were waited for; matrix products, arithmetic and copies ran while one was open for 24% of the time, Pallas kernels for 0%

profile of v1, /device:TPU:0, one launch (start us, length us, event | category | flops | bytes accessed | tf_op | source)
XLA Modules:
  0.0 276.7 jit_solution(12103862402360429610)
XLA Ops:
  7.2 4.9 %collective-permute-start.8 = (bf16[1,72,4096]{2,1,0:T(8,128)(2,1)}, bf16[1,72,4096]{2,1,0:T(8,128)(2,1)S(1)}, u32[]{:S(2)}, u32[]{:S(2)}) collective-permute-start(bf16[1,72,4096]{2,1,0:T(8,128)(2,1)} %param.12), channel_id=1, source_target_pairs={{0,8},{8,16},{16,24},{1,9},{9,17},{17,25},{2,10},{10,18},{18,26},{... | collective-permute-start | bytes 1769480 | tf_op jit(solution)/shard_map/ppermute | solution.py:28
  12.1 3.4 %collective-permute-start = (bf16[1,72,4096]{2,1,0:T(8,128)(2,1)}, bf16[1,72,4096]{2,1,0:T(8,128)(2,1)S(1)}, u32[]{:S(2)}, u32[]{:S(2)}) collective-permute-start(bf16[1,72,4096]{2,1,0:T(8,128)(2,1)} %param.11), channel_id=1, source_target_pairs={{0,8},{8,16},{16,24},{1,9},{9,17},{17,25},{2,10},{10,18},{18,26},{... | collective-permute-start | bytes 1769480 | tf_op jit(solution)/shard_map/ppermute | solution.py:28
  15.5 10.6 %collective-permute-done.8 = bf16[1,72,4096]{2,1,0:T(8,128)(2,1)S(1)} collective-permute-done((bf16[1,72,4096]{2,1,0:T(8,128)(2,1)}, bf16[1,72,4096]{2,1,0:T(8,128)(2,1)S(1)}, u32[]{:S(2)}, u32[]{:S(2)}) %collective-permute-start.8) | collective-permute-done | bytes 589856 | tf_op jit(solution)/shard_map/ppermute | solution.py:28
  26.1 1.9 broadcast_select_fusion
  29.6 7.9 %collective-permute-done = bf16[1,72,4096]{2,1,0:T(8,128)(2,1)S(1)} collective-permute-done((bf16[1,72,4096]{2,1,0:T(8,128)(2,1)}, bf16[1,72,4096]{2,1,0:T(8,128)(2,1)S(1)}, u32[]{:S(2)}, u32[]{:S(2)}) %collective-permute-start) | collective-permute-done | bytes 589856 | tf_op jit(solution)/shard_map/ppermute | solution.py:28
  37.6 1.4 fusion.23
  39.1 2.7 broadcast_in_dim.40
  42.9 3.5 %collective-permute-start.2 = (bf16[72,4096]{1,0:T(8,128)(2,1)S(1)}, bf16[72,4096]{1,0:T(8,128)(2,1)S(1)}, u32[]{:S(2)}, u32[]{:S(2)}) collective-permute-start(bf16[72,4096]{1,0:T(8,128)(2,1)S(1)} %get-tuple-element.7), channel_id=1, source_target_pairs={{0,7},{1,0},{2,1},{3,2},{4,3},{5,4},{6,5},{7,6},{8,15},{9,8},{10,9... | collective-permute-start | bytes 1769480 | tf_op jit(solution)/shard_map/ppermute | solution.py:18
  46.5 47.7 %all-gather.1 = f32[8,72,16]{1,2,0:T(8,128)S(1)} all-gather(f32[1,72,16]{1,2,0:T(8,128)S(1)} %maximum_bitcast_fusion), channel_id=1, replica_groups=mesh['section'=4,'expert'=8] {'expert'}, dimensions={0}, use_global_device_ids=true | all-gather | bytes 41472 | tf_op jit(solution)/shard_map/all_gather | solution.py:65
  94.8 3.2 %collective-permute-start.4 = (bf16[72,4096]{1,0:T(8,128)(2,1)S(1)}, bf16[72,4096]{1,0:T(8,128)(2,1)S(1)}, u32[]{:S(2)}, u32[]{:S(2)}) collective-permute-start(bf16[72,4096]{1,0:T(8,128)(2,1)S(1)} %collective-permute-done.2), channel_id=1, source_target_pairs={{0,7},{1,0},{2,1},{3,2},{4,3},{5,4},{6,5},{7,6},{8,15},{9,8},{10,9... | collective-permute-start | bytes 1769480 | tf_op jit(solution)/shard_map/ppermute | solution.py:18
  99.8 11.8 %collective-permute-done.3 = bf16[72,4096]{1,0:T(8,128)(2,1)S(1)} collective-permute-done((bf16[72,4096]{1,0:T(8,128)(2,1)S(1)}, bf16[72,4096]{1,0:T(8,128)(2,1)S(1)}, u32[]{:S(2)}, u32[]{:S(2)}) %collective-permute-start.3) | collective-permute-done | bytes 589856 | tf_op jit(solution)/shard_map/ppermute | solution.py:15
  111.7 3.5 %collective-permute-start.6 = (bf16[72,4096]{1,0:T(8,128)(2,1)S(1)}, bf16[72,4096]{1,0:T(8,128)(2,1)S(1)}, u32[]{:S(2)}, u32[]{:S(2)}) collective-permute-start(bf16[72,4096]{1,0:T(8,128)(2,1)S(1)} %collective-permute-done.4), channel_id=1, source_target_pairs={{0,7},{1,0},{2,1},{3,2},{4,3},{5,4},{6,5},{7,6},{8,15},{9,8},{10,9... | collective-permute-start | bytes 1769480 | tf_op jit(solution)/shard_map/ppermute | solution.py:18
  117.0 10.8 %collective-permute-done.5 = bf16[72,4096]{1,0:T(8,128)(2,1)S(1)} collective-permute-done((bf16[72,4096]{1,0:T(8,128)(2,1)S(1)}, bf16[72,4096]{1,0:T(8,128)(2,1)S(1)}, u32[]{:S(2)}, u32[]{:S(2)}) %collective-permute-start.5) | collective-permute-done | bytes 589856 | tf_op jit(solution)/shard_map/ppermute | solution.py:15
  129.6 9.4 %collective-permute-done.7 = bf16[72,4096]{1,0:T(8,128)(2,1)S(1)} collective-permute-done((bf16[72,4096]{1,0:T(8,128)(2,1)S(1)}, bf16[72,4096]{1,0:T(8,128)(2,1)S(1)}, u32[]{:S(2)}, u32[]{:S(2)}) %collective-permute-start.7) | collective-permute-done | bytes 589856 | tf_op jit(solution)/shard_map/ppermute | solution.py:15
  139.8 12.1 %fusion.2 = f32[576,1536]{1,0:T(8,128)S(1)} fusion(bf16[576,4096]{1,0:T(8,128)(2,1)} %constant_dynamic-update-slice_fusion, bf16[1,1,4096,1536]{3,2,1,0:T(8,128)(2,1)} %param.20), kind=kOutput, calls=%fused_computation.2 | convolution fusion | flops 7247757312 | bytes 20840448 | tf_op jit(solution)/shard_map/dot_general | solution.py:82
  151.9 5.6 %multiply_convert_fusion = bf16[576,4096]{1,0:T(8,128)(2,1)} fusion(bf16[1,1,768,4096]{3,2,1,0:T(8,128)(2,1)S(1)} %bitcast.63, f32[576]{0:T(1024)S(1)} %get-tuple-element.5, f32[576,1536]{1,0:T(8,128)S(1)} %fusion.2), kind=kOutput, calls=%fused_computation.6 | convolution fusion | flops 3631251456 | bytes 14551296 | tf_op jit(solution)/shard_map/dot_general | solution.py:86
  159.4 2.5 fusion.34
  161.9 9.4 %fusion.16 = (bf16[576,768]{1,0:T(8,128)(2,1)S(1)}, bf16[576,768]{1,0:T(8,128)(2,1)S(1)}) fusion(f32[576,1536]{1,0:T(8,128)} %bitcast.56, bf16[1,1,768,4096]{3,2,1,0:T(8,128)(2,1)} %param.21, bf16[1,576,4096]{2,1,0:T(8,128)(2,1)} %all-gather.4.cloned.1.call-done, f32[576]{0:T(1024)S(1)} %get-tuple-element.4), kind=kOutput, calls=%fused_computation.16 | convolution fusion | flops 3636707328 | bytes 16320768 | tf_op jit(solution)/shard_map/dot_general | solution.py:105
  171.3 18.5 %fusion.8 = bf16[576,4096]{1,0:T(8,128)(2,1)} fusion(bf16[1,1,4096,1536]{3,2,1,0:T(8,128)(2,1)} %param.20, bf16[576,768]{1,0:T(8,128)(2,1)S(1)} %get-tuple-element.11, bf16[576,768]{1,0:T(8,128)(2,1)S(1)} %get-tuple-element.10), kind=kOutput, calls=%fused_computation.10 | convolution fusion | flops 7253655552 | bytes 19070976 | tf_op jit(solution)/shard_map/dot_general | solution.py:113
  189.8 20.9 %reduce-scatter.3.cloned.1.call-done = bf16[72,4096]{1,0:T(8,128)(2,1)} async-done(((bf16[576,4096]{1,0:T(8,128)(2,1)}), bf16[72,4096]{1,0:T(8,128)(2,1)}) %reduce-scatter.3.cloned.1.call-update) | async-done | bytes 589840 | tf_op jit(solution)/shard_map/reduce_scatter | solution.py:88
  210.7 2.0 fusion.31
  212.7 53.6 %reduce-scatter.5.cloned.1.call-done = bf16[72,4096]{1,0:T(8,128)(2,1)} async-done(((bf16[576,4096]{1,0:T(8,128)(2,1)}), bf16[72,4096]{1,0:T(8,128)(2,1)}) %reduce-scatter.5.cloned.1.call-update) | async-done | bytes 589840 | tf_op jit(solution)/shard_map/reduce_scatter | solution.py:116
  266.4 1.4 fusion.27
  267.8 2.3 fusion.32
  (61 shorter events, 11.3 us)
Async XLA Ops:
  7.2 154.7 %all-gather.4.cloned.1.call-start = ((), (), s32[]{:S(2)}) async-start(), calls=%async_computation.4 | async-start | bytes 5308416 | tf_op jit(solution)/shard_map/all_gather | solution.py:81
  7.2 18.9 %collective-permute-start.8 = (bf16[1,72,4096]{2,1,0:T(8,128)(2,1)}, bf16[1,72,4096]{2,1,0:T(8,128)(2,1)S(1)}, u32[]{:S(2)}, u32[]{:S(2)}) collective-permute-start(bf16[1,72,4096]{2,1,0:T(8,128)(2,1)} %param.12), channel_id=1, source_target_pairs={{0,8},{8,16},{16,24},{1,9},{9,17},{17,25},{2,10},{10,18},{18,26},{... | collective-permute-start | bytes 1769480 | tf_op jit(solution)/shard_map/ppermute | solution.py:28
  12.1 25.5 %collective-permute-start = (bf16[1,72,4096]{2,1,0:T(8,128)(2,1)}, bf16[1,72,4096]{2,1,0:T(8,128)(2,1)S(1)}, u32[]{:S(2)}, u32[]{:S(2)}) collective-permute-start(bf16[1,72,4096]{2,1,0:T(8,128)(2,1)} %param.11), channel_id=1, source_target_pairs={{0,8},{8,16},{16,24},{1,9},{9,17},{17,25},{2,10},{10,18},{18,26},{... | collective-permute-start | bytes 1769480 | tf_op jit(solution)/shard_map/ppermute | solution.py:28
  28.0 13.8 %copy-start.3 = (f32[1,4096]{1,0:T(1,128)S(1)}, f32[1,4096]{1,0:T(1,128)}, u32[]{:S(2)}) copy-start(f32[1,4096]{1,0:T(1,128)} %param.15) | copy-start | bytes 49156
  28.1 182.7 %reduce-scatter.3.cloned.1.call-start = ((), (), s32[]{:S(2)}) async-start(), calls=%async_computation.2 | async-start | bytes 5308416 | tf_op jit(solution)/shard_map/reduce_scatter | solution.py:88
  39.0 7.4 %copy-start.4 = (f32[1,72,4]{1,2,0:T(4,128)S(1)}, f32[1,72,4]{1,2,0:T(4,128)}, u32[]{:S(2)}) copy-start(f32[1,72,4]{1,2,0:T(4,128)} %param.19) | copy-start | bytes 3460
  39.0 7.4 %copy-start.5 = (f32[1,72,4]{1,2,0:T(4,128)S(1)}, f32[1,72,4]{1,2,0:T(4,128)}, u32[]{:S(2)}) copy-start(f32[1,72,4]{1,2,0:T(4,128)} %param.17) | copy-start | bytes 3460
  39.0 7.4 %copy-start.6 = (s32[1,72,4]{1,2,0:T(4,128)S(1)}, s32[1,72,4]{1,2,0:T(4,128)}, u32[]{:S(2)}) copy-start(s32[1,72,4]{1,2,0:T(4,128)} %param.18) | copy-start | bytes 3460
  39.0 7.4 %copy-start.7 = (s32[1,72,4]{1,2,0:T(4,128)S(1)}, s32[1,72,4]{1,2,0:T(4,128)}, u32[]{:S(2)}) copy-start(s32[1,72,4]{1,2,0:T(4,128)} %param.16) | copy-start | bytes 3460
  42.9 51.5 %collective-permute-start.1 = (bf16[72,4096]{1,0:T(8,128)(2,1)S(1)}, bf16[72,4096]{1,0:T(8,128)(2,1)S(1)}, u32[]{:S(2)}, u32[]{:S(2)}) collective-permute-start(bf16[72,4096]{1,0:T(8,128)(2,1)S(1)} %get-tuple-element.7), channel_id=1, source_target_pairs={{0,1},{1,2},{2,3},{3,4},{4,5},{5,6},{6,7},{7,0},{8,9},{9,10},{10,1... | collective-permute-start | bytes 1769480 | tf_op jit(solution)/shard_map/ppermute | solution.py:15
  42.9 51.9 %collective-permute-start.2 = (bf16[72,4096]{1,0:T(8,128)(2,1)S(1)}, bf16[72,4096]{1,0:T(8,128)(2,1)S(1)}, u32[]{:S(2)}, u32[]{:S(2)}) collective-permute-start(bf16[72,4096]{1,0:T(8,128)(2,1)S(1)} %get-tuple-element.7), channel_id=1, source_target_pairs={{0,7},{1,0},{2,1},{3,2},{4,3},{5,4},{6,5},{7,6},{8,15},{9,8},{10,9... | collective-permute-start | bytes 1769480 | tf_op jit(solution)/shard_map/ppermute | solution.py:18
  94.4 17.2 %collective-permute-start.3 = (bf16[72,4096]{1,0:T(8,128)(2,1)S(1)}, bf16[72,4096]{1,0:T(8,128)(2,1)S(1)}, u32[]{:S(2)}, u32[]{:S(2)}) collective-permute-start(bf16[72,4096]{1,0:T(8,128)(2,1)S(1)} %collective-permute-done.1), channel_id=1, source_target_pairs={{0,1},{1,2},{2,3},{3,4},{4,5},{5,6},{6,7},{7,0},{8,9},{9,10},{10,1... | collective-permute-start | bytes 1769480 | tf_op jit(solution)/shard_map/ppermute | solution.py:15
  94.8 16.9 %collective-permute-start.4 = (bf16[72,4096]{1,0:T(8,128)(2,1)S(1)}, bf16[72,4096]{1,0:T(8,128)(2,1)S(1)}, u32[]{:S(2)}, u32[]{:S(2)}) collective-permute-start(bf16[72,4096]{1,0:T(8,128)(2,1)S(1)} %collective-permute-done.2), channel_id=1, source_target_pairs={{0,7},{1,0},{2,1},{3,2},{4,3},{5,4},{6,5},{7,6},{8,15},{9,8},{10,9... | collective-permute-start | bytes 1769480 | tf_op jit(solution)/shard_map/ppermute | solution.py:18
  111.7 16.2 %collective-permute-start.5 = (bf16[72,4096]{1,0:T(8,128)(2,1)S(1)}, bf16[72,4096]{1,0:T(8,128)(2,1)S(1)}, u32[]{:S(2)}, u32[]{:S(2)}) collective-permute-start(bf16[72,4096]{1,0:T(8,128)(2,1)S(1)} %collective-permute-done.3), channel_id=1, source_target_pairs={{0,1},{1,2},{2,3},{3,4},{4,5},{5,6},{6,7},{7,0},{8,9},{9,10},{10,1... | collective-permute-start | bytes 1769480 | tf_op jit(solution)/shard_map/ppermute | solution.py:15
  111.7 17.0 %collective-permute-start.6 = (bf16[72,4096]{1,0:T(8,128)(2,1)S(1)}, bf16[72,4096]{1,0:T(8,128)(2,1)S(1)}, u32[]{:S(2)}, u32[]{:S(2)}) collective-permute-start(bf16[72,4096]{1,0:T(8,128)(2,1)S(1)} %collective-permute-done.4), channel_id=1, source_target_pairs={{0,7},{1,0},{2,1},{3,2},{4,3},{5,4},{6,5},{7,6},{8,15},{9,8},{10,9... | collective-permute-start | bytes 1769480 | tf_op jit(solution)/shard_map/ppermute | solution.py:18
  127.8 11.1 %collective-permute-start.7 = (bf16[72,4096]{1,0:T(8,128)(2,1)S(1)}, bf16[72,4096]{1,0:T(8,128)(2,1)S(1)}, u32[]{:S(2)}, u32[]{:S(2)}) collective-permute-start(bf16[72,4096]{1,0:T(8,128)(2,1)S(1)} %collective-permute-done.5), channel_id=1, source_target_pairs={{0,1},{1,2},{2,3},{3,4},{4,5},{5,6},{6,7},{7,0},{8,9},{9,10},{10,1... | collective-permute-start | bytes 1769480 | tf_op jit(solution)/shard_map/ppermute | solution.py:15
  138.9 12.9 %slice-start = ((s8[6291456]{0:T(1024)(128)(4,1)}), s8[4194304]{0:T(1024)(128)(4,1)S(1)}, s32[]{:S(2)}) async-start(s8[6291456]{0:T(1024)(128)(4,1)} %bitcast.62), calls=%async_computation.5 | async-start | bytes 8388608
  139.8 12.1 %slice-start.1 = ((s8[6291456]{0:T(1024)(128)(4,1)}), s8[2097152]{0:T(1024)(128)(4,1)S(1)}, s32[]{:S(2)}) async-start(s8[6291456]{0:T(1024)(128)(4,1)} %bitcast.62), calls=%async_computation.6 | async-start | bytes 4194304
  157.5 1.2 copy-start.2
  157.5 108.9 %reduce-scatter.5.cloned.1.call-start = ((), (), s32[]{:S(2)}) async-start(), calls=%async_computation.3 | async-start | bytes 5308416 | tf_op jit(solution)/shard_map/reduce_scatter | solution.py:116
  189.8 76.6 %copy-start.1 = (bf16[1,72,4096]{2,1,0:T(8,128)(2,1)S(1)}, bf16[1,72,4096]{2,1,0:T(8,128)(2,1)}, u32[]{:S(2)}) copy-start(bf16[1,72,4096]{2,1,0:T(8,128)(2,1)} %param.13) | copy-start | bytes 1769476
  189.8 78.0 %copy-start = (bf16[1,72,4096]{2,1,0:T(8,128)(2,1)S(1)}, bf16[1,72,4096]{2,1,0:T(8,128)(2,1)}, u32[]{:S(2)}) copy-start(bf16[1,72,4096]{2,1,0:T(8,128)(2,1)} %broadcast_select_fusion) | copy-start | bytes 1769476
Sparse Core Ops, SparseCore 0:
  28.2 65.5 all-gather.3
  157.6 53.0 reduce-scatter.2
  213.0 53.3 reduce-scatter.4
